TPU v7x, 512 devices: a whole 4x8x8 slice. The times are simulated.
512 devices in a mesh: seq: 64 (over y, z), tp: 8 (over x, core).
Axes of the slice: x: 4, y: 8, z: 8, core: 2. Of those that a mesh axis runs over, the one named last changes fastest.
Arguments:
- queries: bfloat16 [16384, 4096], P('seq', 'tp'), may hold values from -6 to 6
- keys: bfloat16 [16384, 4096], P('seq', 'tp'), may hold values from -6 to 6
- values: bfloat16 [16384, 4096], P('seq', 'tp'), may hold values from -6 to 6
- out_cotangent: bfloat16 [16384, 2048], P('seq', 'tp'), may hold values from -16 to 16
- proj_weight: bfloat16 [4096, 2048], P('tp', 'seq'), may hold values from -0.125 to 0.125
Outputs:
- grad_queries: bfloat16 [16384, 4096], P('seq', 'tp')
- grad_keys: bfloat16 [16384, 4096], P('seq', 'tp')
- grad_values: bfloat16 [16384, 4096], P('seq', 'tp')
- grad_proj: float32 [4096, 2048], P('tp', 'seq')
All inputs are finite; a program needn't handle non-finite values.
Results may differ from a plain program's by a relative error of at most 0.0058.
Values may be sent and summed in bfloat16 or wider, within the bound.
No kernel may reach another device: no remote copies, remote signals or barrier semaphores. Data moves between devices by JAX's collectives and lax.ppermute only.
A program may use at most 128 MiB of HBM per device.

v0:
```python
import jax
import jax.numpy as jnp
from jax import lax
from jax.sharding import PartitionSpec as P

DH = 128


def entering(part, axis, combine, identity, reverse):
    count = lax.axis_size(axis)
    place = lax.axis_index(axis)
    ahead = count - 1 - place if reverse else place
    gathered = lax.all_gather(part, axis)
    state = jnp.zeros_like(part) + jnp.asarray(identity, part.dtype)

    def one(step, state):
        source = count - 1 - step if reverse else step
        return combine(state, lax.dynamic_index_in_dim(gathered, source, 0, False))

    return lax.fori_loop(0, ahead, one, state)


def add_pair(earlier, later_one):
    return earlier + later_one


def per_device(queries, keys, values, out_cotangent, proj_weight):
    tok = queries.shape[0]
    heads = queries.shape[1] // DH
    seq_count = lax.axis_size("seq")
    scale = 1.0 / jnp.sqrt(jnp.float32(DH * tok * seq_count))
    q_heads = queries.reshape(tok, heads, DH)
    k_heads = keys.reshape(tok, heads, DH)
    v_heads = values.reshape(tok, heads, DH)
    kv_state = jnp.einsum("thd,the->hde", k_heads, v_heads, preferred_element_type=jnp.float32)
    zero_state = jnp.zeros_like(kv_state)
    prior_sum = entering(kv_state, "seq", add_pair, zero_state, False)
    full_cot = lax.all_gather(out_cotangent, "tp", axis=1, tiled=True)
    grad_out = lax.dot_general(
        full_cot,
        lax.all_gather(proj_weight, "seq", axis=1, tiled=True),
        (((1,), (1,)), ((), ())),
        preferred_element_type=jnp.float32,
    ).astype(jnp.bfloat16)
    g_heads = grad_out.reshape(tok, heads, DH)
    qg_state = jnp.einsum("thd,the->hde", q_heads, g_heads, preferred_element_type=jnp.float32)
    later_sum = entering(qg_state, "seq", add_pair, zero_state, True)
    prior = prior_sum.astype(jnp.bfloat16)
    later = later_sum.astype(jnp.bfloat16)
    rows = jnp.arange(tok)
    causal = (rows[:, None] >= rows[None, :])[None]
    attn = jnp.where(
        causal,
        jnp.einsum("thd,shd->hts", q_heads, k_heads, preferred_element_type=jnp.float32),
        0.0,
    ).astype(jnp.bfloat16)
    back = jnp.where(
        causal,
        jnp.einsum("thd,shd->hts", g_heads, v_heads, preferred_element_type=jnp.float32),
        0.0,
    ).astype(jnp.bfloat16)
    attn_out = scale * (
        jnp.einsum("hts,she->the", attn, v_heads, preferred_element_type=jnp.float32)
        + jnp.einsum("thd,hde->the", q_heads, prior, preferred_element_type=jnp.float32)
    )
    grad_q = scale * (
        jnp.einsum("hts,shd->thd", back, k_heads, preferred_element_type=jnp.float32)
        + jnp.einsum("the,hde->thd", g_heads, prior, preferred_element_type=jnp.float32)
    )
    grad_k = scale * (
        jnp.einsum("hts,thd->shd", back, q_heads, preferred_element_type=jnp.float32)
        + jnp.einsum("she,hde->shd", v_heads, later, preferred_element_type=jnp.float32)
    )
    grad_v = scale * (
        jnp.einsum("hts,the->she", attn, g_heads, preferred_element_type=jnp.float32)
        + jnp.einsum("shd,hde->she", k_heads, later, preferred_element_type=jnp.float32)
    )
    out_flat = attn_out.astype(jnp.bfloat16).reshape(tok, heads * DH)
    proj_term = lax.dot_general(
        out_flat, full_cot, (((0,), (0,)), ((), ())), preferred_element_type=jnp.float32
    )
    proj_sum = lax.psum_scatter(proj_term, "seq", scatter_dimension=1, tiled=True)
    grad_proj = proj_sum / jnp.sqrt(jnp.float32(tok * seq_count))
    width = heads * DH
    return (
        grad_q.astype(jnp.bfloat16).reshape(tok, width),
        grad_k.astype(jnp.bfloat16).reshape(tok, width),
        grad_v.astype(jnp.bfloat16).reshape(tok, width),
        grad_proj,
    )


def solution(mesh):
    return jax.shard_map(
        per_device,
        mesh=mesh,
        in_specs=(P("seq", "tp"), P("seq", "tp"), P("seq", "tp"), P("seq", "tp"), P("tp", "seq")),
        out_specs=(P("seq", "tp"), P("seq", "tp"), P("seq", "tp"), P("tp", "seq")),
        check_vma=False,
    )
```

profile of v0, /device:TPU:2, one launch (start us, length us, event | category | flops | bytes accessed | tf_op | source)
XLA Modules:
  0.0 670.4 jit_solution(11894771848935743379)
XLA Ops:
  8.7 1.1 copy.56
  9.8 1.9 fusion.17
  11.8 31.1 %all-gather.7.cloned.1.call-done = bf16[256,2048]{1,0:T(8,128)(2,1)} async-done(((bf16[256,256]{1,0:T(8,128)(2,1)}), bf16[256,2048]{1,0:T(8,128)(2,1)}) %all-gather.7.cloned.1.call-update) | async-done | bytes 1048592 | tf_op jit(solution)/shard_map/all_gather | solution.py:38
  42.9 88.4 %all-gather.9.cloned.1.call-done = bf16[512,2048]{0,1:T(8,128)(2,1)} async-done(((bf16[512,32]{0,1:T(8,128)(2,1)}), bf16[512,2048]{0,1:T(8,128)(2,1)}) %all-gather.9.cloned.1.call-update) | async-done | bytes 2097168 | tf_op jit(solution)/shard_map/all_gather | solution.py:41
  131.3 2.6 convolution_convert_fusion
  135.9 135.8 %all-gather.11.cloned.1.call-done = f32[256,128,128]{2,1,0:T(8,128)} async-done(((f32[4,128,128]{2,1,0:T(8,128)}), f32[256,128,128]{2,1,0:T(8,128)}) %all-gather.11.cloned.1.call-update) | async-done | bytes 16777232 | tf_op jit(solution)/shard_map/all_gather | solution.py:13
  272.1 2.7 fusion.35
  277.1 136.3 %all-gather.13.cloned.1.call-done = f32[256,128,128]{2,1,0:T(8,128)} async-done(((f32[4,128,128]{2,1,0:T(8,128)}), f32[256,128,128]{2,1,0:T(8,128)}) %all-gather.13.cloned.1.call-update) | async-done | bytes 16777232 | tf_op jit(solution)/shard_map/all_gather | solution.py:13
  413.4 65.1 %while.23 = (s32[]{:T(128)}, f32[4,128,128]{2,1,0:T(8,128)S(1)}, s32[]{:T(128)}, f32[64,4,128,128]{3,2,1,0:T(8,128)}, s32[]{:T(128)}, /*index=5*/s32[]{:T(128)}, s32[]{:T(128)}, s32[]{:T(128)}) while((s32[]{:T(128)}, f32[4,128,128]{2,1,0:T(8,128)S(1)}, s32[]{:T(128)}, f32[64,4,128,128]{3,2,1,0:T(8,128)}, s32[]{:T(128)}, /*index=5*/s32[]{:T(128)}, ...), condition=%wide.region_3.4_spmd, body=%wide.region_2.3_spmd.sunk | while | flops 65542 | bytes 786575 | solution.py:20
  429.9 1.0 bitcast_add_fusion.5
  435.1 1.0 bitcast_add_fusion.5
  436.1 1.0 bitcast_add_fusion.5
  440.3 1.0 bitcast_add_fusion.5
  441.3 1.0 bitcast_add_fusion.5
  443.4 1.0 bitcast_add_fusion.5
  447.5 1.0 bitcast_add_fusion.5
  449.6 1.0 bitcast_add_fusion.5
  453.7 1.0 bitcast_add_fusion.5
  456.8 1.0 bitcast_add_fusion.5
  461.0 1.0 bitcast_add_fusion.5
  464.1 1.0 bitcast_add_fusion.5
  473.4 1.0 bitcast_add_fusion.5
  480.7 181.7 %reduce-scatter.2.cloned.1.call-done = f32[512,32]{0,1:T(8,128)} async-done(((f32[512,2048]{0,1:T(8,128)}), f32[512,32]{0,1:T(8,128)}) %reduce-scatter.2.cloned.1.call-update) | async-done | bytes 65552 | tf_op jit(solution)/shard_map/reduce_scatter | solution.py:82
  662.4 1.5 broadcast_multiply_fusion
  (86 shorter events, 58.7 us)
Async XLA Ops:
  7.2 126.9 %copy-start = (bf16[256,512]{1,0:T(8,128)(2,1)S(1)}, bf16[256,512]{1,0:T(8,128)(2,1)}, u32[]{:S(2)}) copy-start(bf16[256,512]{1,0:T(8,128)(2,1)} %param.9) | copy-start | bytes 786436
  7.2 128.1 %copy-start.1 = (bf16[256,512]{1,0:T(8,128)(2,1)S(1)}, bf16[256,512]{1,0:T(8,128)(2,1)}, u32[]{:S(2)}) copy-start(bf16[256,512]{1,0:T(8,128)(2,1)} %param.10) | copy-start | bytes 786436
  7.2 35.7 %all-gather.7.cloned.1.call-start = ((), (), s32[]{:S(2)}) async-start(), calls=%async_computation.1 | async-start | bytes 1179648 | tf_op jit(solution)/shard_map/all_gather | solution.py:38
  7.9 123.4 %all-gather.9.cloned.1.call-start = ((), (), s32[]{:S(2)}) async-start(), calls=%async_computation.2 | async-start | bytes 2129920 | tf_op jit(solution)/shard_map/all_gather | solution.py:41
  8.7 263.1 %all-gather.11.cloned.1.call-start = ((), (), s32[]{:S(2)}) async-start(), calls=%async_computation.4 | async-start | bytes 17039360 | tf_op jit(solution)/shard_map/all_gather | solution.py:13
  11.8 401.6 %all-gather.13.cloned.1.call-start = ((), (), s32[]{:S(2)}) async-start(), calls=%async_computation.5 | async-start | bytes 17039360 | tf_op jit(solution)/shard_map/all_gather | solution.py:13
  135.2 527.2 %reduce-scatter.2.cloned.1.call-start = ((), (), s32[]{:S(2)}) async-start(), calls=%async_computation.3 | async-start | bytes 4259840 | tf_op jit(solution)/shard_map/reduce_scatter | solution.py:82
  135.3 136.8 %copy-start.2 = (bf16[256,2048]{1,0:T(8,128)(2,1)S(1)}, bf16[256,2048]{1,0:T(8,128)(2,1)}, u32[]{:S(2)}) copy-start(bf16[256,2048]{1,0:T(8,128)(2,1)} %all-gather.7.cloned.1.call-done) | copy-start | bytes 3145732
Sparse Core Ops, SparseCore 0:
  10.1 32.7 all-gather.6
  45.9 85.3 all-gather.8
  134.9 136.7 all-gather.10
  275.2 138.1 all-gather.12
  417.3 245.0 reduce-scatter.1
where the time goes:
time: 673 us; the launch traced here: 670 us
  waiting for transfers between devices  575 us (85%)
  other arithmetic  65.2 us (10%)
  between operations  13.9 us (2%)
  matrix products  10.2 us (2%)
    all_gather x2, waiting for transfers between devices, entering(): gathered = lax.all_gather(part, axis)  272 us
    reduce_scatter x1, waiting for transfers between devices, per_device(): lax.psum_scatter(proj_term, 'seq', scatter_dimension=1, tiled=True)  182 us
    all_gather x1, waiting for transfers between devices, per_device(): lax.all_gather(proj_weight, 'seq', axis=1, tiled=True)  88.4 us
    add x63, other arithmetic, add_pair(): return earlier + later_one  63.7 us
    all_gather x1, waiting for transfers between devices, per_device(): full_cot = lax.all_gather(out_cotangent, 'tp', axis=1, tiled=True)  31.1 us
  transfers between devices with their start and end apart: 5, of which 5 were waited for; matrix products, arithmetic and copies ran while one was open for 12% of the time, Pallas kernels for 0%

commit v1 on v0

--- a/solution.py
+++ b/solution.py
@@ -35,7 +35,27 @@
     kv_state = jnp.einsum("thd,the->hde", k_heads, v_heads, preferred_element_type=jnp.float32)
     zero_state = jnp.zeros_like(kv_state)
     prior_sum = entering(kv_state, "seq", add_pair, zero_state, False)
-    full_cot = lax.all_gather(out_cotangent, "tp", axis=1, tiled=True)
+    count_2, place_2, extent = (lax.axis_size("tp"), lax.axis_index("tp"), out_cotangent.shape[1])
+    right = [(i, (i + 1) % count_2) for i in range(count_2)]
+    backward = [(i, (i - 1) % count_2) for i in range(count_2)]
+    filled = jnp.zeros(
+        (*out_cotangent.shape[:1], count_2 * extent, *out_cotangent.shape[1 + 1 :]),
+        out_cotangent.dtype,
+    )
+    filled = lax.dynamic_update_slice_in_dim(filled, out_cotangent, place_2 * extent, axis=1)
+    from_left = from_right = out_cotangent
+    middle = count_2 // 2
+    for step_2 in range(1, middle + 1):
+        from_left = lax.ppermute(from_left, "tp", right)
+        filled = lax.dynamic_update_slice_in_dim(
+            filled, from_left, (place_2 - step_2) % count_2 * extent, axis=1
+        )
+        if step_2 < count_2 - middle:
+            from_right = lax.ppermute(from_right, "tp", backward)
+            filled = lax.dynamic_update_slice_in_dim(
+                filled, from_right, (place_2 + step_2) % count_2 * extent, axis=1
+            )
+    full_cot = filled
     grad_out = lax.dot_general(
         full_cot,
         lax.all_gather(proj_weight, "seq", axis=1, tiled=True),

time: 673 us -> 641 us (0.952)
  waiting for transfers between devices: 575 us -> 535 us
  starting transfers between devices: 0.2 us -> 7.56 us
    all_gather x1 -> x0, waiting for transfers between devices: 31.1 us -> none  [per_device(): full_cot = lax.all_gather(out_cotangent, 'tp', axis=1, tiled=True)]
    all_gather x1, waiting for transfers between devices: 88.4 us -> 67.4 us  [per_device(): lax.all_gather(proj_weight, 'seq', axis=1, tiled=True)]
    ppermute x0 -> x7, waiting for transfers between devices: none -> 12.3 us  [the longest x4 12.3 us: per_device(): from_left = lax.ppermute(from_left, 'tp', right)]
    ppermute x0 -> x7, starting transfers between devices: none -> 7.4 us  [the longest x3 7.37 us: per_device(): from_right = lax.ppermute(from_right, 'tp', backward)]
  transfers between devices with their start and end apart: 5 -> 11, of which waited for: 5 -> 8; matrix products, arithmetic and copies ran while one was open for 12% -> 12% of each run, Pallas kernels for 0% -> 0%
where the time goes in v1:
time: 641 us; the launch traced here: 639 us
  waiting for transfers between devices  535 us (83%)
  other arithmetic  65.2 us (10%)
  between operations  14 us (2%)
  matrix products  9.87 us (2%)
  starting transfers between devices  7.56 us (1%)
    all_gather x2, waiting for transfers between devices, entering(): gathered = lax.all_gather(part, axis)  273 us
    reduce_scatter x1, waiting for transfers between devices, per_device(): lax.psum_scatter(proj_term, 'seq', scatter_dimension=1, tiled=True)  181 us
    all_gather x1, waiting for transfers between devices, per_device(): lax.all_gather(proj_weight, 'seq', axis=1, tiled=True)  67.4 us
    add x63, other arithmetic, add_pair(): return earlier + later_one  63.7 us
  transfers between devices with their start and end apart: 11, of which 8 were waited for; matrix products, arithmetic and copies ran while one was open for 12% of the time, Pallas kernels for 0%

profile of v1, /device:TPU:2, one launch (start us, length us, event | category | flops | bytes accessed | tf_op | source)
XLA Modules:
  0.0 638.7 jit_solution(18164911491396075937)
XLA Ops:
  8.0 1.1 copy.56
  9.1 1.9 fusion.17
  11.1 1.7 collective-permute-start.1
  13.9 1.8 collective-permute-done
  15.7 2.6 collective-permute-start.3
  18.4 2.5 collective-permute-done.2
  20.9 3.0 collective-permute-start.5
  23.9 2.5 collective-permute-done.4
  26.5 5.5 collective-permute-done.6
  32.0 67.4 %all-gather.6.cloned.1.call-done = bf16[512,2048]{0,1:T(8,128)(2,1)} async-done(((bf16[512,32]{0,1:T(8,128)(2,1)}), bf16[512,2048]{0,1:T(8,128)(2,1)}) %all-gather.6.cloned.1.call-update) | async-done | bytes 2097168 | tf_op jit(solution)/shard_map/all_gather | solution.py:61
  99.5 2.3 convolution_convert_fusion
  103.7 136.2 %all-gather.8.cloned.1.call-done = f32[256,128,128]{2,1,0:T(8,128)} async-done(((f32[4,128,128]{2,1,0:T(8,128)}), f32[256,128,128]{2,1,0:T(8,128)}) %all-gather.8.cloned.1.call-update) | async-done | bytes 16777232 | tf_op jit(solution)/shard_map/all_gather | solution.py:13
  240.2 2.7 fusion.35
  245.1 136.5 %all-gather.10.cloned.1.call-done = f32[256,128,128]{2,1,0:T(8,128)} async-done(((f32[4,128,128]{2,1,0:T(8,128)}), f32[256,128,128]{2,1,0:T(8,128)}) %all-gather.10.cloned.1.call-update) | async-done | bytes 16777232 | tf_op jit(solution)/shard_map/all_gather | solution.py:13
  381.6 65.4 %while.23 = (s32[]{:T(128)}, f32[4,128,128]{2,1,0:T(8,128)S(1)}, s32[]{:T(128)}, f32[64,4,128,128]{3,2,1,0:T(8,128)}, s32[]{:T(128)}, /*index=5*/s32[]{:T(128)}, s32[]{:T(128)}, s32[]{:T(128)}) while((s32[]{:T(128)}, f32[4,128,128]{2,1,0:T(8,128)S(1)}, s32[]{:T(128)}, f32[64,4,128,128]{3,2,1,0:T(8,128)}, s32[]{:T(128)}, /*index=5*/s32[]{:T(128)}, ...), condition=%wide.region_3.4_spmd, body=%wide.region_2.3_spmd.sunk | while | flops 65542 | bytes 786567 | solution.py:20
  398.3 1.0 bitcast_add_fusion.5
  404.5 1.0 bitcast_add_fusion.5
  408.6 1.0 bitcast_add_fusion.5
  409.7 1.0 bitcast_add_fusion.5
  411.8 1.0 bitcast_add_fusion.5
  425.3 1.0 bitcast_add_fusion.5
  426.3 1.0 bitcast_add_fusion.5
  449.3 181.5 %reduce-scatter.2.cloned.1.call-done = f32[512,32]{0,1:T(8,128)} async-done(((f32[512,2048]{0,1:T(8,128)}), f32[512,32]{0,1:T(8,128)}) %reduce-scatter.2.cloned.1.call-update) | async-done | bytes 65552 | tf_op jit(solution)/shard_map/reduce_scatter | solution.py:102
  630.7 1.5 broadcast_multiply_fusion
  (104 shorter events, 65.2 us)
Async XLA Ops:
  7.2 94.7 %copy-start = (bf16[256,512]{1,0:T(8,128)(2,1)S(1)}, bf16[256,512]{1,0:T(8,128)(2,1)}, u32[]{:S(2)}) copy-start(bf16[256,512]{1,0:T(8,128)(2,1)} %param.9) | copy-start | bytes 786436
  7.2 92.3 %all-gather.6.cloned.1.call-start = ((), (), s32[]{:S(2)}) async-start(), calls=%async_computation.1 | async-start | bytes 2129920 | tf_op jit(solution)/shard_map/all_gather | solution.py:61
  7.9 231.9 %all-gather.8.cloned.1.call-start = ((), (), s32[]{:S(2)}) async-start(), calls=%async_computation.3 | async-start | bytes 17039360 | tf_op jit(solution)/shard_map/all_gather | solution.py:13
  11.0 370.6 %all-gather.10.cloned.1.call-start = ((), (), s32[]{:S(2)}) async-start(), calls=%async_computation.4 | async-start | bytes 17039360 | tf_op jit(solution)/shard_map/all_gather | solution.py:13
  11.1 4.6 collective-permute-start
  11.1 4.6 collective-permute-start.1
  12.9 90.1 %copy-start.1 = (bf16[256,512]{1,0:T(8,128)(2,1)S(1)}, bf16[256,512]{1,0:T(8,128)(2,1)}, u32[]{:S(2)}) copy-start(bf16[256,512]{1,0:T(8,128)(2,1)} %param.10) | copy-start | bytes 786436
  15.7 5.2 collective-permute-start.2
  15.7 5.2 collective-permute-start.3
  20.9 5.5 collective-permute-start.4
  20.9 5.5 collective-permute-start.5
  26.4 5.6 collective-permute-start.6
  103.0 527.8 %reduce-scatter.2.cloned.1.call-start = ((), (), s32[]{:S(2)}) async-start(), calls=%async_computation.2 | async-start | bytes 4259840 | tf_op jit(solution)/shard_map/reduce_scatter | solution.py:102
Sparse Core Ops, SparseCore 0:
  11.0 88.3 all-gather.5
  103.0 136.7 all-gather.7
  243.4 138.1 all-gather.9
  385.5 245.1 reduce-scatter.1
